TPU v7x, 256 devices: a whole 4x4x8 slice. The times are simulated.
256 devices in a mesh: dp: 2 (over x_lo), context: 8 (over z), tensor: 16 (over y, x_hi, core).
Axes of the slice: x: 4 (x_hi: 2, x_lo: 2; x = x_hi * 2 + x_lo), y: 4, z: 8, core: 2. Of those that a mesh axis runs over, the one named last changes fastest.
Arguments:
- activations: bfloat16 [2, 4096, 4096], P('dp', ('context', 'tensor')), may hold values from -60 to 60
- in_weight: bfloat16 [4096, 3, 4096], P('dp', None, 'tensor'), may hold values from -0.09375 to 0.09375
- out_weight: bfloat16 [4096, 4096], P('tensor', 'dp'), may hold values from -0.09375 to 0.09375
- short_filter: float32 [3, 3, 4096], P(None, None, 'tensor'), may hold values from -2 to 2
- mixer_filter: float32 [128, 256], P(None, 'tensor'), may hold values from -0.5 to 0.5
- cotangent: bfloat16 [2, 4096, 4096], P('dp', ('context', 'tensor')), may hold values from -6 to 6
Outputs:
- block_out: bfloat16 [2, 4096, 4096], P('dp', ('context', 'tensor'))
- grad_input: bfloat16 [2, 4096, 4096], P('dp', ('context', 'tensor'))
- grad_in_weight: bfloat16 [4096, 3, 4096], P(('dp', 'context'), None, 'tensor')
- grad_out_weight: bfloat16 [4096, 4096], P('tensor', ('dp', 'context'))
- grad_short: float32 [3, 3, 4096], P(None, None, 'tensor')
- grad_mixer: float32 [128, 256], P(None, 'tensor')
All inputs are finite; a program needn't handle non-finite values.
Results may differ from a plain program's by a relative error of at most 0.019.
Values may be sent and summed in bfloat16 or wider, within the bound.
A program may use at most 128 MiB of HBM per device.

v0:
```python
import jax
import jax.numpy as jnp
from jax import lax
from jax.sharding import PartitionSpec as P

EPS = 1e-05


def from_behind(value, axis, steps):
    count = lax.axis_size(axis)
    initial, last = (max(0, -steps), min(count, count - steps))
    return lax.ppermute(value, axis, [(source, source + steps) for source in range(initial, last)])


def skew_table(base, span):
    groups = base.shape[0]
    padded = jnp.concatenate([base, jnp.zeros((groups, span + 1), jnp.float32)], axis=1)
    tiled = jnp.tile(padded[:, None, :], (1, span, 1)).reshape(groups, span * (2 * span + 1))
    return tiled[:, : span * 2 * span].reshape(groups, span, 2 * span)


def band_windows(extended, span, groups):
    chans = extended.shape[1]
    padded = jnp.concatenate([extended, jnp.zeros((1, chans), jnp.float32)], 0)
    blocks = padded.shape[0] // span
    padded = padded.reshape(blocks, span, groups, chans // groups)
    return jnp.concatenate([padded[:-1], padded[1:]], axis=1)


def band_apply(table, extended, span):
    groups = table.shape[0]
    chans = extended.shape[1]
    windows = band_windows(extended, span, groups)
    result = jnp.einsum("gtu,bugc->btgc", table, windows, precision=lax.Precision.HIGHEST)
    return result.reshape(windows.shape[0] * span, chans)


def band_grad(left, extended, span, groups):
    rows, chans = left.shape
    lhs = left.reshape(rows // span, span, groups, chans // groups)
    windows = band_windows(extended, span, groups)
    prods = jnp.einsum("btgc,bugc->gtu", lhs, windows, precision=lax.Precision.HIGHEST)
    flat = jnp.concatenate(
        [prods.reshape(groups, span * 2 * span), jnp.zeros((groups, span), jnp.float32)], axis=1
    )
    skewed = flat.reshape(groups, span, 2 * span + 1).sum(axis=1)
    return jnp.flip(skewed[:, :span], axis=1).T


def short_apply(filters, extended, rows):
    taps = filters.shape[1]
    total = jnp.zeros((rows,) + extended.shape[1:], jnp.float32)
    for tap in range(taps):
        total = total + filters[:, tap][None] * extended[taps - 1 - tap : taps - 1 - tap + rows]
    return total


def per_device(activations, in_weight, out_weight, short_filter, mixer_filter, cotangent):
    rows_own = activations.shape[1]
    width = activations.shape[2]
    rows = rows_own * lax.axis_size("tensor")
    span = mixer_filter.shape[0]
    groups = mixer_filter.shape[1]
    taps = short_filter.shape[1]
    chans = short_filter.shape[2]
    own = activations[0].astype(jnp.float32)
    inverse = lax.rsqrt(jnp.mean(own * own, axis=-1, keepdims=True) + EPS)
    normed = (own * inverse).astype(jnp.bfloat16)
    slab = lax.all_gather(normed, "tensor", axis=0, tiled=True)
    full_in, full_out = (
        lax.all_gather(in_weight, "dp", axis=0, tiled=True),
        lax.all_gather(out_weight, "dp", axis=1, tiled=True),
    )
    in_flat = full_in.reshape(width, 3 * chans)
    projected = (
        jnp.dot(slab, in_flat, preferred_element_type=jnp.float32)
        .astype(jnp.bfloat16)
        .reshape(rows, 3, chans)
    )
    proj_wide = projected.astype(jnp.float32)
    table_fwd = skew_table(jnp.flip(mixer_filter, axis=0).T, span)
    table_back = skew_table(mixer_filter.T, span)
    short_rim = from_behind(projected[rows - taps + 1 :], "context", 1)
    proj_ext = jnp.concatenate([short_rim.astype(jnp.float32), proj_wide], 0)
    streams = short_apply(short_filter, proj_ext, rows)
    gated = (streams[:, 1] * streams[:, 2]).astype(jnp.bfloat16)
    gate_rim = from_behind(gated[rows - span + 1 :], "context", 1)
    gate_ext = jnp.concatenate([gate_rim, gated], 0).astype(jnp.float32)
    mixed = band_apply(table_fwd, gate_ext, span)
    output_rows = (streams[:, 0] * mixed).astype(jnp.bfloat16)
    piece = output_rows
    branch = lax.psum_scatter(
        jnp.dot(piece, full_out, preferred_element_type=jnp.float32).astype(jnp.bfloat16),
        "tensor",
        scatter_dimension=0,
        tiled=True,
    ).astype(jnp.float32)
    block_out = (own + branch).astype(jnp.bfloat16)[None]
    cot_slab = lax.all_gather(cotangent[0], "tensor", axis=0, tiled=True)
    grad_rows = lax.dot_general(
        cot_slab, full_out, (((1,), (1,)), ((), ())), preferred_element_type=jnp.float32
    )
    out_term = lax.dot_general(
        output_rows, cot_slab, (((0,), (0,)), ((), ())), preferred_element_type=jnp.float32
    )
    grad_mix = (grad_rows * streams[:, 0]).astype(jnp.bfloat16)
    grad_mix_wide = grad_mix.astype(jnp.float32)
    mix_rim = from_behind(grad_mix[: span - 1], "context", -1)
    grad_gate = band_apply(
        table_back, jnp.concatenate([grad_mix_wide, mix_rim.astype(jnp.float32)], 0), span
    )
    mixer_term = band_grad(grad_mix_wide, gate_ext, span, groups)
    grad_streams = jnp.stack(
        [grad_rows * mixed, grad_gate * streams[:, 2], grad_gate * streams[:, 1]], axis=1
    )
    stream_rim = from_behind(grad_streams[: taps - 1], "context", -1)
    stream_ext = jnp.concatenate([grad_streams, stream_rim], 0)
    grad_proj = jnp.zeros((rows, 3, chans), jnp.float32)
    for tap in range(taps):
        grad_proj = grad_proj + short_filter[:, tap][None] * stream_ext[tap : tap + rows]
    grad_proj = grad_proj.astype(jnp.bfloat16)
    short_terms = [
        jnp.sum(grad_streams * proj_ext[taps - 1 - tap : taps - 1 - tap + rows], axis=0)
        for tap in range(taps)
    ]
    short_term = jnp.stack(short_terms, axis=1)
    grad_short, grad_mixer = lax.psum((short_term, mixer_term), ("dp", "context"))
    proj_flat = grad_proj.reshape(rows, 3 * chans)
    in_term = lax.dot_general(
        slab, proj_flat, (((0,), (0,)), ((), ())), preferred_element_type=jnp.float32
    ).reshape(width, 3, chans)
    grad_in, grad_out = (
        lax.psum_scatter(
            in_term.astype(jnp.bfloat16), ("dp", "context"), scatter_dimension=0, tiled=True
        ).astype(jnp.float32),
        lax.psum_scatter(
            out_term.astype(jnp.bfloat16), ("dp", "context"), scatter_dimension=1, tiled=True
        ).astype(jnp.float32),
    )
    piece = proj_flat
    grad_norm = lax.psum_scatter(
        lax.dot_general(
            piece, in_flat, (((1,), (1,)), ((), ())), preferred_element_type=jnp.float32
        ).astype(jnp.bfloat16),
        "tensor",
        scatter_dimension=0,
        tiled=True,
    ).astype(jnp.float32)
    grad_x = (
        cotangent[0].astype(jnp.float32)
        + inverse * grad_norm
        - own * inverse**3 * jnp.mean(grad_norm * own, axis=-1, keepdims=True)
    )
    grad_input = grad_x.astype(jnp.bfloat16)[None]
    return (
        block_out,
        grad_input,
        grad_in.astype(jnp.bfloat16),
        grad_out.astype(jnp.bfloat16),
        grad_short,
        grad_mixer,
    )


def solution(mesh):
    placed = (
        P("dp", ("context", "tensor"), None),
        P("dp", None, "tensor"),
        P("tensor", "dp"),
        P(None, None, "tensor"),
        P(None, "tensor"),
        P("dp", ("context", "tensor"), None),
    )
    return jax.shard_map(
        per_device,
        mesh=mesh,
        in_specs=placed,
        out_specs=(
            P("dp", ("context", "tensor"), None),
            P("dp", ("context", "tensor"), None),
            P(("dp", "context"), None, "tensor"),
            P("tensor", ("dp", "context")),
            P(None, None, "tensor"),
            P(None, "tensor"),
        ),
        check_vma=False,
    )
```

profile of v0, /device:TPU:8, one launch (start us, length us, event | category | flops | bytes accessed | tf_op | source)
XLA Modules:
  0.0 682.4 jit_solution(12522044125238099399)
XLA Ops:
  10.5 87.6 %all-gather.8.cloned.1.call-done = bf16[4096,3,256]{2,0,1:T(8,128)(2,1)} async-done(((bf16[2048,3,256]{2,0,1:T(8,128)(2,1)}), bf16[4096,3,256]{2,0,1:T(8,128)(2,1)}) %all-gather.8.cloned.1.call-update) | async-done | bytes 6291472 | tf_op jit(solution)/shard_map/all_gather | solution.py:71
  98.1 8.7 %copy.20 = bf16[4096,3,256]{0,2,1:T(8,128)(2,1)} copy(bf16[4096,3,256]{2,0,1:T(8,128)(2,1)} %all-gather.8.cloned.1.call-done) | data formatting | bytes 12582912 | tf_op jit(solution)/shard_map/all_gather | solution.py:71
  106.8 54.3 %all-gather.6.cloned.1.call-done = bf16[512,4096]{1,0:T(8,128)(2,1)} async-done(((bf16[32,4096]{1,0:T(8,128)(2,1)}), bf16[512,4096]{1,0:T(8,128)(2,1)}) %all-gather.6.cloned.1.call-update) | async-done | bytes 4194320 | tf_op jit(solution)/shard_map/all_gather | solution.py:69
  161.1 7.5 %convolution_convert_fusion.3 = bf16[512,768]{1,0:T(8,128)(2,1)S(1)} fusion(bf16[512,4096]{1,0:T(8,128)(2,1)} %all-gather.6.cloned.1.call-done, bf16[4096,768]{0,1:T(8,128)(2,1)} %bitcast.133), kind=kOutput, calls=%fused_computation.27 | convolution fusion | flops 3221618688 | bytes 11272192 | tf_op jit(solution)/shard_map/dot_general | solution.py:76
  168.6 3.5 collective-permute-start
  173.9 26.4 %all-gather.10.cloned.1.call-done = bf16[256,4096]{1,0:T(8,128)(2,1)} async-done(((bf16[256,2048]{1,0:T(8,128)(2,1)}), bf16[256,4096]{1,0:T(8,128)(2,1)}) %all-gather.10.cloned.1.call-update) | async-done | bytes 2097168 | tf_op jit(solution)/shard_map/all_gather | solution.py:72
  200.3 62.2 %all-gather.12.cloned.1.call-done = bf16[1,512,4096]{2,1,0:T(8,128)(2,1)} async-done(((bf16[1,32,4096]{2,1,0:T(8,128)(2,1)}), bf16[1,512,4096]{2,1,0:T(8,128)(2,1)}) %all-gather.12.cloned.1.call-update) | async-done | bytes 4194320 | tf_op jit(solution)/shard_map/all_gather | solution.py:99
  262.5 5.2 fusion.36
  269.8 1.9 tile.16
  271.8 3.9 tile.17
  277.2 2.0 copy.53
  283.1 3.9 fusion.15
  289.7 4.7 collective-permute-start.1
  294.5 1.9 tile.14
  296.4 3.9 tile.15
  301.9 2.0 copy.51
  304.9 2.0 copy.26
  306.9 2.1 slice.105
  310.0 2.0 slice.103
  313.8 2.3 fusion.12
  320.7 4.2 collective-permute-done.3
  327.0 5.1 bitcast_convert_fusion
  333.6 3.3 convolution_convert_fusion.1
  337.0 4.8 convolution_convert_fusion.2
  343.3 8.6 %convolution_convert_fusion = bf16[4096,3,256]{2,0,1:T(8,128)(2,1)} fusion(bf16[512,4096]{1,0:T(8,128)(2,1)} %all-gather.6.cloned.1.call-done, bf16[512,3,256]{0,2,1:T(8,128)(2,1)S(1)} %copy.39), kind=kOutput, calls=%fused_computation.1 | convolution fusion | flops 3224371200 | bytes 11272192 | tf_op jit(solution)/shard_map/dot_general | solution.py:129
  358.9 3.7 reshape.99
  362.9 1.9 copy.41
  365.1 62.9 %all-reduce.4 = (f32[3,3,256]{2,0,1:T(4,128)S(1)}, f32[128,16]{0,1:T(8,128)}) all-reduce(f32[3,3,256]{2,0,1:T(4,128)S(1)} %pad_maximum_fusion.4, f32[128,16]{0,1:T(8,128)S(1)} %bitcast.141), channel_id=1, replica_groups=mesh['dp'=2,'context'=8,'tensor'=16] {'dp','context'}, use_global_device_ids=true, to_apply=%region_9.10 | all-reduce | flops 4352 | bytes 34816 | tf_op jit(solution)/shard_map/psum | solution.py:127
  429.8 81.3 %reduce-scatter.5.cloned.1.call-done = bf16[32,4096]{1,0:T(8,128)(2,1)} async-done(((bf16[512,4096]{1,0:T(8,128)(2,1)}), bf16[32,4096]{1,0:T(8,128)(2,1)}) %reduce-scatter.5.cloned.1.call-update) | async-done | bytes 262160 | tf_op jit(solution)/shard_map/reduce_scatter | solution.py:92
  511.0 2.0 fusion.32
  513.1 75.3 %reduce-scatter.11.cloned.1.call-done = bf16[256,256]{1,0:T(8,128)(2,1)} async-done(((bf16[256,4096]{1,0:T(8,128)(2,1)}), bf16[256,256]{1,0:T(8,128)(2,1)}) %reduce-scatter.11.cloned.1.call-update) | async-done | bytes 131088 | tf_op jit(solution)/shard_map/reduce_scatter | solution.py:136
  588.4 87.1 %reduce-scatter.9.cloned.1.call-done = bf16[256,3,256]{2,0,1:T(8,128)(2,1)} async-done(((bf16[4096,3,256]{2,0,1:T(8,128)(2,1)}), bf16[256,3,256]{2,0,1:T(8,128)(2,1)}) %reduce-scatter.9.cloned.1.call-update) | async-done | bytes 393232 | tf_op jit(solution)/shard_map/reduce_scatter | solution.py:133
  (132 shorter events, 39.4 us)
Async XLA Ops:
  7.2 90.9 %all-gather.8.cloned.1.call-start = ((), (), s32[]{:S(2)}) async-start(), calls=%async_computation.5 | async-start | bytes 9437184 | tf_op jit(solution)/shard_map/all_gather | solution.py:71
  7.9 2.6 copy-start.20
  7.9 153.2 %all-gather.6.cloned.1.call-start = ((), (), s32[]{:S(2)}) async-start(), calls=%async_computation.4 | async-start | bytes 4456448 | tf_op jit(solution)/shard_map/all_gather | solution.py:69
  9.1 191.1 %all-gather.10.cloned.1.call-start = ((), (), s32[]{:S(2)}) async-start(), calls=%async_computation.6 | async-start | bytes 3145728 | tf_op jit(solution)/shard_map/all_gather | solution.py:72
  9.9 252.6 %all-gather.12.cloned.1.call-start = ((), (), s32[]{:S(2)}) async-start(), calls=%async_computation.11 | async-start | bytes 4456448 | tf_op jit(solution)/shard_map/all_gather | solution.py:99
  10.5 418.2 %reduce-scatter.7.cloned.1.call-start = ((), (), s32[]{:S(2)}) async-start(), calls=%async_computation.8 | async-start | bytes 4456448 | tf_op jit(solution)/shard_map/reduce_scatter | solution.py:141
  168.6 3.8 copy-start.7
  168.6 4.8 collective-permute-start
  173.9 93.9 %copy-start.5 = (f32[512,3,256]{2,0,1:T(8,128)}, f32[512,3,256]{2,0,1:T(8,128)S(1)}, u32[]{:S(2)}) copy-start(f32[512,3,256]{2,0,1:T(8,128)S(1)} %multiply_add_fusion) | copy-start | bytes 4718596
  173.9 96.0 %copy-start.19 = (f32[128,16]{0,1:T(8,128)S(1)}, f32[128,16]{0,1:T(8,128)}, u32[]{:S(2)}) copy-start(f32[128,16]{0,1:T(8,128)} %param.10) | copy-start | bytes 24580
  268.5 11.2 %collective-permute-start.2 = (bf16[127,256]{1,0:T(8,128)(2,1)S(1)}, bf16[127,256]{1,0:T(8,128)(2,1)S(1)}, u32[]{:S(2)}, u32[]{:S(2)}) collective-permute-start(bf16[127,256]{1,0:T(8,128)(2,1)S(1)} %slice.125), channel_id=1, source_target_pairs={{16,0},{32,16},{48,32},{64,48},{80,64},{96,80},{112,96},{17,1},{33... | collective-permute-start | bytes 195080 | tf_op jit(solution)/shard_map/ppermute | solution.py:12
  275.6 1.6 slice-start
  277.2 2.0 copy-start.14
  289.7 14.2 %collective-permute-start.1 = (bf16[127,256]{1,0:T(8,128)(2,1)S(1)}, bf16[127,256]{1,0:T(8,128)(2,1)S(1)}, u32[]{:S(2)}, u32[]{:S(2)}) collective-permute-start(bf16[127,256]{1,0:T(8,128)(2,1)S(1)} %slice_bitcast_fusion.1), channel_id=1, source_target_pairs={{0,16},{16,32},{32,48},{48,64},{64,80},{80,96},{96,112},{1,17},{17... | collective-permute-start | bytes 195080 | tf_op jit(solution)/shard_map/ppermute | solution.py:12
  300.3 1.6 slice-start.1
  301.9 2.0 copy-start.17
  310.0 3.3 copy-start.12
  312.0 1.7 copy-start
  313.4 2.7 copy-start.1
  317.4 9.6 %slice-start.2 = ((s8[6291456]{0:T(1024)(128)(4,1)}), s8[4194304]{0:T(1024)(128)(4,1)S(1)}, s32[]{:S(2)}) async-start(s8[6291456]{0:T(1024)(128)(4,1)} %bitcast.131), calls=%async_computation.14 | async-start | bytes 8388608
  319.1 1.6 copy-start.3
  319.1 7.8 %slice-start.3 = ((s8[6291456]{0:T(1024)(128)(4,1)}), s8[2097152]{0:T(1024)(128)(4,1)S(1)}, s32[]{:S(2)}) async-start(s8[6291456]{0:T(1024)(128)(4,1)} %bitcast.131), calls=%async_computation.15 | async-start | bytes 4194304
  319.1 5.8 collective-permute-start.3
  332.0 1.6 copy-start.11
  332.1 179.0 %reduce-scatter.5.cloned.1.call-start = ((), (), s32[]{:S(2)}) async-start(), calls=%async_computation.7 | async-start | bytes 4456448 | tf_op jit(solution)/shard_map/reduce_scatter | solution.py:92
  336.9 251.5 %reduce-scatter.11.cloned.1.call-start = ((), (), s32[]{:S(2)}) async-start(), calls=%async_computation.10 | async-start | bytes 2228224 | tf_op jit(solution)/shard_map/reduce_scatter | solution.py:136
  341.8 1.2 copy-start.10
  341.8 333.7 %reduce-scatter.9.cloned.1.call-start = ((), (), s32[]{:S(2)}) async-start(), calls=%async_computation.9 | async-start | bytes 6684672 | tf_op jit(solution)/shard_map/reduce_scatter | solution.py:133
  351.8 1.6 copy-start.4
  353.5 1.6 copy-start.2
  362.8 2.0 copy-start.8
  364.8 146.2 %copy-start.18 = (bf16[1,32,4096]{2,1,0:T(8,128)(2,1)S(1)}, bf16[1,32,4096]{2,1,0:T(8,128)(2,1)}, u32[]{:S(2)}) copy-start(bf16[1,32,4096]{2,1,0:T(8,128)(2,1)} %param.11) | copy-start | bytes 786436
  (5 other events, 4.3 us)
Sparse Core Ops, SparseCore 0:
  9.8 88.2 all-gather.7
  101.4 59.5 all-gather.5
  162.9 37.3 all-gather.9
  202.9 59.5 all-gather.11
  332.2 87.3 reduce-scatter.6
  423.8 87.2 reduce-scatter.4
  514.1 74.2 reduce-scatter.10
  591.5 83.9 reduce-scatter.8
where the time goes:
time: 683 us; the launch traced here: 682 us
  waiting for transfers between devices  481 us (70%)
  blocking collectives  62.9 us (9%)
  local copies, waits for them, and re-layouts  60.3 us (9%)
  matrix products  41.7 us (6%)
  between operations  14.6 us (2%)
  starting transfers between devices  11.6 us (2%)
  other arithmetic  10.4 us (2%)
    all_gather x1, waiting for transfers between devices, per_device(): lax.all_gather(in_weight, 'dp', axis=0, tiled=True)  87.6 us
    reduce_scatter x1, waiting for transfers between devices, per_device(): lax.psum_scatter(in_term.astype(jnp.bfloat16), ('dp', 'context'), scatter...  87.1 us
    reduce_scatter x1, waiting for transfers between devices, per_device(): lax.psum_scatter(jnp.dot(piece, full_out, preferred_element_type=jnp.floa...  81.3 us
    reduce_scatter x1, waiting for transfers between devices, per_device(): lax.psum_scatter(out_term.astype(jnp.bfloat16), ('dp', 'context'), scatte...  75.3 us
    psum x1, blocking collectives, per_device(): lax.psum((short_term, mixer_term), ('dp', 'context'))  62.9 us
    all_gather x1, waiting for transfers between devices, per_device(): cot_slab = lax.all_gather(cotangent[0], 'tensor', axis=0, tiled=True)  62.2 us
    all_gather x1, waiting for transfers between devices, per_device(): slab = lax.all_gather(normed, 'tensor', axis=0, tiled=True)  54.3 us
    all_gather x1, waiting for transfers between devices, per_device(): lax.all_gather(out_weight, 'dp', axis=1, tiled=True)  26.4 us
  transfers between devices with their start and end apart: 12, of which 9 were waited for; matrix products, arithmetic and copies ran while one was open for 10% of the time, Pallas kernels for 0%

commit v1 on v0

--- a/solution.py
+++ b/solution.py
@@ -66,7 +66,15 @@
     own = activations[0].astype(jnp.float32)
     inverse = lax.rsqrt(jnp.mean(own * own, axis=-1, keepdims=True) + EPS)
     normed = (own * inverse).astype(jnp.bfloat16)
-    slab = lax.all_gather(normed, "tensor", axis=0, tiled=True)
+    slab = jnp.concatenate(
+        jax.lax.all_to_all(
+            jnp.stack(tuple((normed for _ in range(jax.lax.axis_size("tensor"))))),
+            axis_name="tensor",
+            split_axis=0,
+            concat_axis=0,
+        ),
+        0,
+    )
     full_in, full_out = (
         lax.all_gather(in_weight, "dp", axis=0, tiled=True),
         lax.all_gather(out_weight, "dp", axis=1, tiled=True),

time: 683 us -> 661 us (0.968)
  waiting for transfers between devices: 481 us -> 449 us
  starting transfers between devices: 11.6 us -> 19.4 us
    all_gather x1 -> x0, waiting for transfers between devices: 54.3 us -> none  [per_device(): slab = lax.all_gather(normed, 'tensor', axis=0, tiled=True)]
    all_gather x1, waiting for transfers between devices: 87.6 us -> 114 us  [per_device(): lax.all_gather(in_weight, 'dp', axis=0, tiled=True)]
    all_to_all x0 -> x1, starting transfers between devices: none -> 7.52 us  [per_device(): jax.lax.all_to_all(jnp.stack(tuple((normed for _ in range(jax.lax.axis_si...]
  transfers between devices with their start and end apart: 12 -> 12, of which waited for: 9 -> 8; matrix products, arithmetic and copies ran while one was open for 10% -> 10% of each run, Pallas kernels for 0% -> 0%
where the time goes in v1:
time: 661 us; the launch traced here: 659 us
  waiting for transfers between devices  449 us (68%)
  blocking collectives  62.9 us (10%)
  local copies, waits for them, and re-layouts  62.6 us (9%)
  matrix products  41.6 us (6%)
  starting transfers between devices  19.4 us (3%)
  between operations  14.6 us (2%)
  other arithmetic  9.66 us (1%)
    all_gather x1, waiting for transfers between devices, per_device(): lax.all_gather(in_weight, 'dp', axis=0, tiled=True)  114 us
    reduce_scatter x1, waiting for transfers between devices, per_device(): lax.psum_scatter(in_term.astype(jnp.bfloat16), ('dp', 'context'), scatter...  87.3 us
    reduce_scatter x1, waiting for transfers between devices, per_device(): lax.psum_scatter(jnp.dot(piece, full_out, preferred_element_type=jnp.floa...  81.3 us
    reduce_scatter x1, waiting for transfers between devices, per_device(): lax.psum_scatter(out_term.astype(jnp.bfloat16), ('dp', 'context'), scatte...  75.3 us
    psum x1, blocking collectives, per_device(): lax.psum((short_term, mixer_term), ('dp', 'context'))  62.9 us
    all_gather x1, waiting for transfers between devices, per_device(): cot_slab = lax.all_gather(cotangent[0], 'tensor', axis=0, tiled=True)  62.4 us
    all_gather x1, waiting for transfers between devices, per_device(): lax.all_gather(out_weight, 'dp', axis=1, tiled=True)  21.5 us
    unnamed x54, local copies, waits for them, and re-layouts  13.9 us
  transfers between devices with their start and end apart: 12, of which 8 were waited for; matrix products, arithmetic and copies ran while one was open for 10% of the time, Pallas kernels for 0%

profile of v1, /device:TPU:8, one launch (start us, length us, event | category | flops | bytes accessed | tf_op | source)
XLA Modules:
  0.0 659.5 jit_solution(5653169715225890364)
XLA Ops:
  9.7 2.5 stack.19
  12.2 7.5 %all-to-all-start = ((bf16[16,32,4096]{2,1,0:T(8,128)(2,1)}), bf16[16,32,4096]{2,1,0:T(8,128)(2,1)}, u32[]{:S(2)}, u32[]{:S(2)}) async-start(bf16[16,32,4096]{2,1,0:T(8,128)(2,1)} %stack.19), calls=%async_computation | async-start | bytes 8388608 | tf_op jit(solution)/shard_map/all_to_all | solution.py:70
  19.8 114.3 %all-gather.5.cloned.1.call-done = bf16[4096,3,256]{2,0,1:T(8,128)(2,1)} async-done(((bf16[2048,3,256]{2,0,1:T(8,128)(2,1)}), bf16[4096,3,256]{2,0,1:T(8,128)(2,1)}) %all-gather.5.cloned.1.call-update) | async-done | bytes 6291472 | tf_op jit(solution)/shard_map/all_gather | solution.py:79
  134.1 8.7 %copy.21 = bf16[4096,3,256]{0,2,1:T(8,128)(2,1)} copy(bf16[4096,3,256]{2,0,1:T(8,128)(2,1)} %all-gather.5.cloned.1.call-done) | data formatting | bytes 12582912 | tf_op jit(solution)/shard_map/all_gather | solution.py:79
  142.8 7.5 %convolution_convert_fusion.3 = bf16[512,768]{1,0:T(8,128)(2,1)S(1)} fusion(bf16[512,4096]{1,0:T(8,128)(2,1)} %bitcast.2, bf16[4096,768]{0,1:T(8,128)(2,1)} %bitcast.153), kind=kOutput, calls=%fused_computation.26 | convolution fusion | flops 3221618688 | bytes 11272192 | tf_op jit(solution)/shard_map/dot_general | solution.py:84
  150.4 3.8 collective-permute-start
  156.0 21.5 %all-gather.7.cloned.1.call-done = bf16[256,4096]{1,0:T(8,128)(2,1)} async-done(((bf16[256,2048]{1,0:T(8,128)(2,1)}), bf16[256,4096]{1,0:T(8,128)(2,1)}) %all-gather.7.cloned.1.call-update) | async-done | bytes 2097168 | tf_op jit(solution)/shard_map/all_gather | solution.py:80
  177.4 62.4 %all-gather.9.cloned.1.call-done = bf16[1,512,4096]{2,1,0:T(8,128)(2,1)} async-done(((bf16[1,32,4096]{2,1,0:T(8,128)(2,1)}), bf16[1,512,4096]{2,1,0:T(8,128)(2,1)}) %all-gather.9.cloned.1.call-update) | async-done | bytes 4194320 | tf_op jit(solution)/shard_map/all_gather | solution.py:107
  239.8 5.2 fusion.40
  249.2 3.9 tile.17
  254.7 2.0 copy.57
  260.5 3.9 fusion.14
  267.1 4.6 collective-permute-start.1
  271.7 1.9 tile.14
  273.6 3.9 tile.15
  279.1 2.0 copy.55
  282.1 2.0 copy.27
  284.1 2.0 slice.105
  287.1 2.1 slice.103
  290.9 2.3 fusion.11
  298.0 4.0 collective-permute-done.3
  304.0 5.0 bitcast_convert_fusion
  310.6 3.3 convolution_convert_fusion.1
  314.0 4.8 convolution_convert_fusion.2
  320.2 8.6 %convolution_convert_fusion = bf16[4096,3,256]{2,0,1:T(8,128)(2,1)} fusion(bf16[512,4096,1]{1,0,2:T(8,128)(2,1)} %bitcast.21, bf16[512,3,256]{0,2,1:T(8,128)(2,1)S(1)} %copy.40), kind=kOutput, calls=%fused_computation.1 | convolution fusion | flops 3224371200 | bytes 11272192 | tf_op jit(solution)/shard_map/dot_general | solution.py:137
  335.9 3.7 reshape.111
  339.9 1.9 copy.43
  342.1 62.9 %all-reduce.4 = (f32[3,3,256]{2,0,1:T(4,128)S(1)}, f32[128,16]{0,1:T(8,128)}) all-reduce(f32[3,3,256]{2,0,1:T(4,128)S(1)} %pad_maximum_fusion.4, f32[128,16]{0,1:T(8,128)S(1)} %bitcast.161), channel_id=1, replica_groups=mesh['dp'=2,'context'=8,'tensor'=16] {'dp','context'}, use_global_device_ids=true, to_apply=%region_9.10 | all-reduce | flops 4352 | bytes 34816 | tf_op jit(solution)/shard_map/psum | solution.py:135
  406.8 81.3 %reduce-scatter.5.cloned.1.call-done = bf16[32,4096]{1,0:T(8,128)(2,1)} async-done(((bf16[512,4096]{1,0:T(8,128)(2,1)}), bf16[32,4096]{1,0:T(8,128)(2,1)}) %reduce-scatter.5.cloned.1.call-update) | async-done | bytes 262160 | tf_op jit(solution)/shard_map/reduce_scatter | solution.py:100
  488.0 2.0 fusion.36
  490.1 75.3 %reduce-scatter.11.cloned.1.call-done = bf16[256,256]{1,0:T(8,128)(2,1)} async-done(((bf16[256,4096]{1,0:T(8,128)(2,1)}), bf16[256,256]{1,0:T(8,128)(2,1)}) %reduce-scatter.11.cloned.1.call-update) | async-done | bytes 131088 | tf_op jit(solution)/shard_map/reduce_scatter | solution.py:144
  565.4 87.3 %reduce-scatter.9.cloned.1.call-done = bf16[256,3,256]{2,0,1:T(8,128)(2,1)} async-done(((bf16[4096,3,256]{2,0,1:T(8,128)(2,1)}), bf16[256,3,256]{2,0,1:T(8,128)(2,1)}) %reduce-scatter.9.cloned.1.call-update) | async-done | bytes 393232 | tf_op jit(solution)/shard_map/reduce_scatter | solution.py:141
  (132 shorter events, 40.8 us)
Async XLA Ops:
  7.2 2.2 copy-start.6
  7.2 127.0 %all-gather.5.cloned.1.call-start = ((), (), s32[]{:S(2)}) async-start(), calls=%async_computation.5 | async-start | bytes 9437184 | tf_op jit(solution)/shard_map/all_gather | solution.py:79
  7.9 169.5 %all-gather.7.cloned.1.call-start = ((), (), s32[]{:S(2)}) async-start(), calls=%async_computation.6 | async-start | bytes 3145728 | tf_op jit(solution)/shard_map/all_gather | solution.py:80
  8.7 231.2 %all-gather.9.cloned.1.call-start = ((), (), s32[]{:S(2)}) async-start(), calls=%async_computation.11 | async-start | bytes 4456448 | tf_op jit(solution)/shard_map/all_gather | solution.py:107
  12.2 7.6 %copy-start.20 = (f32[3,3,256]{2,1,0:T(4,128)S(1)}, f32[3,3,256]{2,1,0:T(4,128)}, u32[]{:S(2)}) copy-start(f32[3,3,256]{2,1,0:T(4,128)} %param.9) | copy-start | bytes 27652
  12.2 130.6 %all-to-all-start = ((bf16[16,32,4096]{2,1,0:T(8,128)(2,1)}), bf16[16,32,4096]{2,1,0:T(8,128)(2,1)}, u32[]{:S(2)}, u32[]{:S(2)}) async-start(bf16[16,32,4096]{2,1,0:T(8,128)(2,1)} %stack.19), calls=%async_computation | async-start | bytes 8388608 | tf_op jit(solution)/shard_map/all_to_all | solution.py:70
  19.8 385.9 %reduce-scatter.7.cloned.1.call-start = ((), (), s32[]{:S(2)}) async-start(), calls=%async_computation.8 | async-start | bytes 4456448 | tf_op jit(solution)/shard_map/reduce_scatter | solution.py:149
  150.3 4.2 copy-start.7
  150.4 5.1 collective-permute-start
  156.0 89.1 %copy-start.5 = (f32[512,3,256]{2,0,1:T(8,128)}, f32[512,3,256]{2,0,1:T(8,128)S(1)}, u32[]{:S(2)}) copy-start(f32[512,3,256]{2,0,1:T(8,128)S(1)} %multiply_add_fusion) | copy-start | bytes 4718596
  156.0 91.4 %copy-start.19 = (f32[128,16]{0,1:T(8,128)S(1)}, f32[128,16]{0,1:T(8,128)}, u32[]{:S(2)}) copy-start(f32[128,16]{0,1:T(8,128)} %param.10) | copy-start | bytes 24580
  245.8 11.3 %collective-permute-start.2 = (bf16[127,256]{1,0:T(8,128)(2,1)S(1)}, bf16[127,256]{1,0:T(8,128)(2,1)S(1)}, u32[]{:S(2)}, u32[]{:S(2)}) collective-permute-start(bf16[127,256]{1,0:T(8,128)(2,1)S(1)} %slice.125), channel_id=1, source_target_pairs={{16,0},{32,16},{48,32},{64,48},{80,64},{96,80},{112,96},{17,1},{33... | collective-permute-start | bytes 195080 | tf_op jit(solution)/shard_map/ppermute | solution.py:12
  253.1 1.6 slice-start
  254.7 2.0 copy-start.14
  267.1 14.0 %collective-permute-start.1 = (bf16[127,256]{1,0:T(8,128)(2,1)S(1)}, bf16[127,256]{1,0:T(8,128)(2,1)S(1)}, u32[]{:S(2)}, u32[]{:S(2)}) collective-permute-start(bf16[127,256]{1,0:T(8,128)(2,1)S(1)} %slice_bitcast_fusion.1), channel_id=1, source_target_pairs={{0,16},{16,32},{32,48},{48,64},{64,80},{80,96},{96,112},{1,17},{17... | collective-permute-start | bytes 195080 | tf_op jit(solution)/shard_map/ppermute | solution.py:12
  277.5 1.6 slice-start.1
  279.1 2.0 copy-start.17
  287.1 3.3 copy-start.12
  289.2 1.7 copy-start
  290.5 2.7 copy-start.1
  294.5 9.5 %slice-start.2 = ((s8[6291456]{0:T(1024)(128)(4,1)}), s8[4194304]{0:T(1024)(128)(4,1)S(1)}, s32[]{:S(2)}) async-start(s8[6291456]{0:T(1024)(128)(4,1)} %bitcast.151), calls=%async_computation.14 | async-start | bytes 8388608
  296.2 1.8 copy-start.3
  296.2 7.8 %slice-start.3 = ((s8[6291456]{0:T(1024)(128)(4,1)}), s8[2097152]{0:T(1024)(128)(4,1)S(1)}, s32[]{:S(2)}) async-start(s8[6291456]{0:T(1024)(128)(4,1)} %bitcast.151), calls=%async_computation.15 | async-start | bytes 4194304
  296.2 5.8 collective-permute-start.3
  309.0 1.6 copy-start.11
  309.1 179.0 %reduce-scatter.5.cloned.1.call-start = ((), (), s32[]{:S(2)}) async-start(), calls=%async_computation.7 | async-start | bytes 4456448 | tf_op jit(solution)/shard_map/reduce_scatter | solution.py:100
  313.9 251.4 %reduce-scatter.11.cloned.1.call-start = ((), (), s32[]{:S(2)}) async-start(), calls=%async_computation.10 | async-start | bytes 2228224 | tf_op jit(solution)/shard_map/reduce_scatter | solution.py:144
  318.8 333.8 %reduce-scatter.9.cloned.1.call-start = ((), (), s32[]{:S(2)}) async-start(), calls=%async_computation.9 | async-start | bytes 6684672 | tf_op jit(solution)/shard_map/reduce_scatter | solution.py:141
  328.8 1.6 copy-start.4
  330.5 1.6 copy-start.2
  339.8 2.0 copy-start.8
  341.8 146.2 %copy-start.18 = (bf16[1,32,4096]{2,1,0:T(8,128)(2,1)S(1)}, bf16[1,32,4096]{2,1,0:T(8,128)(2,1)}, u32[]{:S(2)}) copy-start(bf16[1,32,4096]{2,1,0:T(8,128)(2,1)} %param.11) | copy-start | bytes 786436
  (5 other events, 4.5 us)
Sparse Core Ops, SparseCore 0:
  9.8 124.3 all-gather.4
  135.9 41.4 all-gather.6
  180.2 59.5 all-gather.8
  309.2 87.4 reduce-scatter.6
  400.8 87.2 reduce-scatter.4
  491.0 74.3 reduce-scatter.10
  568.5 84.0 reduce-scatter.8
